TPU v7x, 32 devices: a whole 2x2x4 slice. The times are simulated.
32 devices in a mesh: gx: 4 (over y, x), gy: 8 (over z, core).
Axes of the slice: x: 2, y: 2, z: 4, core: 2. Of those that a mesh axis runs over, the one named last changes fastest.
Arguments:
- material: int32 [8, 128, 512], P('gx', 'gy'), may hold values from 0 to 3
- phase: int32 [8, 128, 512], P('gx', 'gy'), may hold values from 0 to 7
- clock: float32 [1], replicated, may hold values from -3.140625 to 3.140625
- displacement: float32 [3, 8, 128, 512], P(None, 'gx', 'gy'), may hold values from -6 to 6
- velocity: float32 [3, 8, 128, 512], P(None, 'gx', 'gy'), may hold values from -6 to 6
- cotangent: float32 [3, 8, 128, 512], P(None, 'gx', 'gy'), may hold values from -4 to 4
- material_table: float32 [2, 4], replicated, may hold values from 0.5 to 4
- w_in: bfloat16 [256, 10], replicated, may hold values from -2 to 2
- b_in: float32 [256], replicated, may hold values from -3 to 3
- w_mid: bfloat16 [2, 256, 256], replicated, may hold values from -0.375 to 0.375
- b_mid: float32 [2, 256], replicated, may hold values from -3 to 3
- w_out: bfloat16 [9, 256], replicated, may hold values from -0.375 to 0.375
- b_out: float32 [9], replicated, may hold values from -3 to 3
Outputs:
- velocity_new: float32 [3, 8, 128, 512], P(None, 'gx', 'gy')
- displacement_grad: float32 [3, 8, 128, 512], P(None, 'gx', 'gy')
- grad_w_in: float32 [256, 10], replicated
- grad_b_in: float32 [256], replicated
- grad_w_mid: float32 [2, 256, 256], replicated
- grad_b_mid: float32 [2, 256], replicated
- grad_w_out: float32 [9, 256], replicated
- grad_b_out: float32 [9], replicated
All inputs are finite; a program needn't handle non-finite values.
Results may differ from a plain program's by a relative error of at most 0.02.
Values sent between devices are 32-bit elements; how exact they have to be, the bound alone decides.
No kernel may reach another device: no remote copies, remote signals or barrier semaphores. Data moves between devices by JAX's collectives and lax.ppermute only.
A program may use at most 64 MiB of HBM per device.

v0:
```python
import jax
import jax.numpy as jnp
from jax import lax
from jax.sharding import PartitionSpec as P

FEAT = 10
OUT = 9
PHASES = 8
NPARAM = 136713
time_step = 0.25
viscosity = 0.2
norm_eps = 1e-06
two_pi = 6.283185307179586


def with_halo(block, sides, width):
    for axis, dim in sides:
        count = lax.axis_size(axis)
        forward = [(i, i + 1) for i in range(count - 1)]
        backward = [(target, source) for source, target in forward]
        low = lax.ppermute(
            lax.slice_in_dim(block, block.shape[dim] - width, None, axis=dim), axis, forward
        )
        high = lax.ppermute(lax.slice_in_dim(block, 0, width, axis=dim), axis, backward)
        block = jnp.concatenate([low, block, high], axis=dim)
    return block


def zdiff(field):
    padded = jnp.pad(field, ((0, 0), (0, 0), (0, 0), (1, 1)))
    return (padded[..., 2:] - padded[..., :-2]) * 0.5


def xdiff_both(padded):
    return (padded[:, 2:, 1:-1] - padded[:, :-2, 1:-1]) * 0.5


def ydiff_both(padded):
    return (padded[:, 1:-1, 2:] - padded[:, 1:-1, :-2]) * 0.5


def forward_block(feats, w_in, b_in, w_mid, b_mid, w_out, b_out):
    first = jnp.tanh(
        jnp.dot(w_in, feats, preferred_element_type=jnp.float32) + b_in[:, None]
    ).astype(jnp.bfloat16)
    second = jnp.tanh(
        jnp.dot(w_mid[0], first, preferred_element_type=jnp.float32) + b_mid[0][:, None]
    ).astype(jnp.bfloat16)
    third = jnp.tanh(
        jnp.dot(w_mid[1], second, preferred_element_type=jnp.float32) + b_mid[1][:, None]
    ).astype(jnp.bfloat16)
    result = jnp.dot(w_out, third, preferred_element_type=jnp.float32) + b_out[:, None]
    return (first, second, third, result)


def backward_block(feats, delta, w_in, b_in, w_mid, b_mid, w_out, b_out):
    first, second, third, result = forward_block(feats, w_in, b_in, w_mid, b_mid, w_out, b_out)
    delta_out = delta.astype(jnp.bfloat16)
    grad_wout = jnp.dot(delta_out, third.T, preferred_element_type=jnp.float32)
    grad_bout = jnp.sum(delta_out.astype(jnp.float32), axis=1)
    back_third = jnp.dot(w_out.T, delta_out, preferred_element_type=jnp.float32)
    delta_third = (back_third * (1.0 - jnp.square(third.astype(jnp.float32)))).astype(jnp.bfloat16)
    grad_wthree = jnp.dot(delta_third, second.T, preferred_element_type=jnp.float32)
    grad_bthree = jnp.sum(delta_third.astype(jnp.float32), axis=1)
    back_second = jnp.dot(w_mid[1].T, delta_third, preferred_element_type=jnp.float32)
    delta_second = (back_second * (1.0 - jnp.square(second.astype(jnp.float32)))).astype(
        jnp.bfloat16
    )
    grad_wtwo = jnp.dot(delta_second, first.T, preferred_element_type=jnp.float32)
    grad_btwo = jnp.sum(delta_second.astype(jnp.float32), axis=1)
    back_first = jnp.dot(w_mid[0].T, delta_second, preferred_element_type=jnp.float32)
    delta_first = (back_first * (1.0 - jnp.square(first.astype(jnp.float32)))).astype(jnp.bfloat16)
    grad_win = jnp.dot(delta_first, feats.T, preferred_element_type=jnp.float32)
    grad_bin = jnp.sum(delta_first.astype(jnp.float32), axis=1)
    back_feats = jnp.dot(w_in.T, delta_first, preferred_element_type=jnp.float32)
    grads = (
        grad_win,
        grad_bin,
        jnp.stack([grad_wtwo, grad_wthree]),
        jnp.stack([grad_btwo, grad_bthree]),
        grad_wout,
        grad_bout,
    )
    return (grads, back_feats, result)


def body(
    material,
    phase,
    clock,
    displacement,
    velocity,
    cotangent,
    material_table,
    w_in,
    b_in,
    w_mid,
    b_mid,
    w_out,
    b_out,
):
    size_x, size_y, size_z = material.shape
    kinds = jnp.arange(material_table.shape[1], dtype=jnp.int32)
    onehot = (material[None] == kinds[:, None, None, None]).astype(jnp.float32)
    stiffness = jnp.tensordot(material_table[0], onehot, axes=1)
    density = jnp.tensordot(material_table[1], onehot, axes=1)
    occupied = (material > 0).astype(jnp.float32)
    actuation = jnp.sin(two_pi * phase.astype(jnp.float32) / PHASES + clock[0])
    carried = time_step * occupied * cotangent / density
    rims = with_halo(jnp.concatenate([displacement, velocity], 0), (("gx", 1), ("gy", 2)), 1)
    disp_rim = rims[0:3]
    velo_rim = rims[3:6]
    strain = jnp.stack(
        [xdiff_both(disp_rim), ydiff_both(disp_rim), zdiff(displacement)], axis=1
    ).reshape(9, size_x, size_y, size_z)
    feats = jnp.concatenate([strain, actuation[None]], 0).reshape(FEAT, -1).astype(jnp.bfloat16)
    voxels = size_x * size_y * size_z
    block_rows = min(2048, voxels)
    count = voxels // block_rows
    feat_blocks = feats.reshape(FEAT, count, block_rows).transpose(1, 0, 2)
    weights = (w_in, b_in, w_mid, b_mid, w_out, b_out)
    carried_rim = with_halo(carried, (("gx", 1), ("gy", 2)), 1)
    stress_grad = -jnp.stack(
        [xdiff_both(carried_rim), ydiff_both(carried_rim), zdiff(carried)], axis=1
    ).reshape(9, size_x, size_y, size_z)
    delta_all = (
        (occupied * stiffness * stress_grad).reshape(OUT, count, block_rows).transpose(1, 0, 2)
    )
    zeros = (
        jnp.zeros(w_in.shape, jnp.float32),
        jnp.zeros(b_in.shape, jnp.float32),
        jnp.zeros(w_mid.shape, jnp.float32),
        jnp.zeros(b_mid.shape, jnp.float32),
        jnp.zeros(w_out.shape, jnp.float32),
        jnp.zeros(b_out.shape, jnp.float32),
    )

    def backward_step(carry, pieces):
        grads, back_feats, result = backward_block(pieces[0], pieces[1], *weights)
        return (
            jax.tree.map(lambda left, right: left + right, carry, grads),
            (back_feats[:9], result),
        )

    partials, (back_blocks, outputs) = lax.scan(backward_step, zeros, (feat_blocks, delta_all))
    network = outputs.transpose(1, 0, 2).reshape(OUT, size_x, size_y, size_z)
    stress = (occupied * stiffness * network).reshape(3, 3, size_x, size_y, size_z)
    stress_x = with_halo(stress[:, 0], (("gx", 1),), 1)
    stress_y = with_halo(stress[:, 1], (("gy", 2),), 1)
    force = (
        (stress_x[:, 2:] - stress_x[:, :-2]) * 0.5
        + (stress_y[:, :, 2:] - stress_y[:, :, :-2]) * 0.5
        + zdiff(stress[:, 2])
    )
    inner = velo_rim[:, 1:-1, 1:-1]
    lap_z = jnp.pad(velocity, ((0, 0), (0, 0), (0, 0), (1, 1)))
    laplacian = -6.0 * velocity
    laplacian = laplacian + velo_rim[:, 2:, 1:-1] + velo_rim[:, :-2, 1:-1]
    laplacian = laplacian + velo_rim[:, 1:-1, 2:] + velo_rim[:, 1:-1, :-2]
    laplacian = laplacian + lap_z[..., 2:] + lap_z[..., :-2]
    velocity_new = inner + time_step * occupied * (force + viscosity * laplacian) / density
    strain_grad = back_blocks.transpose(1, 0, 2).reshape(3, 3, size_x, size_y, size_z)
    back_x = with_halo(strain_grad[:, 0], (("gx", 1),), 1)
    back_y = with_halo(strain_grad[:, 1], (("gy", 2),), 1)
    displacement_grad = -(
        (back_x[:, 2:] - back_x[:, :-2]) * 0.5
        + (back_y[:, :, 2:] - back_y[:, :, :-2]) * 0.5
        + zdiff(strain_grad[:, 2])
    )
    summed = lax.psum(
        (partials[0], partials[1], partials[2], partials[3], partials[4], partials[5]), ("gx", "gy")
    )
    total = sum((jnp.sum(jnp.square(item)) for item in summed))
    scale = lax.rsqrt(total / NPARAM + norm_eps)
    results = tuple((item * scale for item in summed))
    return (
        velocity_new,
        displacement_grad,
        results[0],
        results[1],
        results[2],
        results[3],
        results[4],
        results[5],
    )


def solution(mesh):
    in_specs = (
        P("gx", "gy", None),
        P("gx", "gy", None),
        P(),
        P(None, "gx", "gy", None),
        P(None, "gx", "gy", None),
        P(None, "gx", "gy", None),
        P(),
        P(),
        P(),
        P(),
        P(),
        P(),
        P(),
    )
    out_specs = (P(None, "gx", "gy", None), P(None, "gx", "gy", None), P(), P(), P(), P(), P(), P())
    return jax.shard_map(body, mesh=mesh, in_specs=in_specs, out_specs=out_specs, check_vma=False)
```

profile of v0, /device:TPU:0, one launch (start us, length us, event | category | flops | bytes accessed | tf_op | source)
XLA Modules:
  0.0 267.0 jit_solution(9475212293226691999)
XLA Ops:
  7.2 0.9 iota_compare_fusion
  8.2 0.9 fusion.70
  9.1 0.9 fusion.72
  10.2 4.8 %collective-permute-start.1 = (f32[3,1,16,512]{3,2,1,0:T(8,128)S(1)}, f32[3,1,16,512]{3,2,1,0:T(8,128)S(1)}, u32[]{:S(2)}, u32[]{:S(2)}) collective-permute-start(f32[3,1,16,512]{3,2,1,0:T(8,128)S(1)} %get-tuple-element.257), channel_id=1, source_target_pairs={{0,8},{8,16},{16,24},{1,9},{9,17},{17,25},{2,10},{10,18},{18,26},{... | collective-permute-start | bytes 294920 | tf_op jit(solution)/shard_map/ppermute | solution.py:21
  15.1 1.4 collective-permute-start
  16.6 0.8 constant_dynamic-update-slice_fusion.1
  17.4 0.8 fusion.78
  18.2 4.5 %collective-permute-start.5 = (f32[6,1,16,512]{3,2,1,0:T(8,128)}, f32[6,1,16,512]{3,2,1,0:T(8,128)S(1)}, u32[]{:S(2)}, u32[]{:S(2)}) collective-permute-start(f32[6,1,16,512]{3,2,1,0:T(8,128)} %get-tuple-element.240), channel_id=1, source_target_pairs={{0,8},{8,16},{16,24},{1,9},{9,17},{17,25},{2,10},{10,18},{18,26},{... | collective-permute-start | bytes 589832 | tf_op jit(solution)/shard_map/ppermute | solution.py:21
  22.7 1.3 collective-permute-start.4
  24.8 1.3 collective-permute-start.2
  26.1 3.0 %collective-permute-start.3 = (f32[3,4,1,512]{3,2,1,0:T(1,128)S(1)}, f32[3,4,1,512]{3,2,1,0:T(1,128)S(1)}, u32[]{:S(2)}, u32[]{:S(2)}) collective-permute-start(f32[3,4,1,512]{3,2,1,0:T(1,128)S(1)} %get-tuple-element.245), channel_id=1, source_target_pairs={{0,1},{1,2},{2,3},{3,4},{4,5},{5,6},{6,7},{8,9},{9,10},{10,11},{11... | collective-permute-start | bytes 73736 | tf_op jit(solution)/shard_map/ppermute | solution.py:21
  31.3 2.3 collective-permute-done.4
  33.7 1.4 collective-permute-start.6
  35.1 3.0 %collective-permute-start.7 = (f32[6,4,1,512]{3,2,1,0:T(1,128)S(1)}, f32[6,4,1,512]{3,2,1,0:T(1,128)S(1)}, u32[]{:S(2)}, u32[]{:S(2)}) collective-permute-start(f32[6,4,1,512]{3,2,1,0:T(1,128)S(1)} %get-tuple-element.233), channel_id=1, source_target_pairs={{0,1},{1,2},{2,3},{3,4},{4,5},{5,6},{6,7},{8,9},{9,10},{10,11},{11... | collective-permute-start | bytes 147464 | tf_op jit(solution)/shard_map/ppermute | solution.py:21
  38.1 0.9 multiply_bitcast_fusion
  40.5 76.0 %while.25 = (s32[]{:T(128)}, f32[256,10]{0,1:T(8,128)S(1)}, f32[256]{0:T(256)}, f32[2,256,256]{2,1,0:T(8,128)S(1)}, f32[2,256]{1,0:T(2,128)}, /*index=5*/f32[9,2...) while((s32[]{:T(128)}, f32[256,10]{0,1:T(8,128)S(1)}, ...), condition=%wide.region_5.6_spmd.clone, body=%wide.region_0.5_spmd.clone.sunk | while | flops 1684996864 | bytes 26539676 | solution.py:145
  42.0 1.2 fusion.149
  49.4 0.8 fusion.150
  50.4 1.2 fusion.153
  51.6 1.2 fusion.149
  60.0 1.2 fusion.153
  61.2 1.2 fusion.149
  69.6 1.2 fusion.153
  70.8 1.2 fusion.149
  79.2 1.2 fusion.153
  80.3 1.2 fusion.149
  88.7 1.2 fusion.153
  89.9 1.2 fusion.149
  98.3 1.2 fusion.153
  99.5 1.2 fusion.149
  107.9 1.2 fusion.153
  109.1 1.2 fusion.149
  118.5 1.3 collective-permute-start.10
  119.9 44.8 %all-reduce.5 = (f32[256,10]{0,1:T(8,128)S(1)}, f32[256]{0:T(256)S(1)}, f32[2,256]{1,0:T(2,128)S(1)}, f32[9,256]{1,0:T(8,128)S(1)}, f32[9]{0:T(128)S(1)}) all-reduce(f32[256,10]{0,1:T(8,128)S(1)} %copy-done.11, f32[256]{0:T(256)S(1)} %copy-done.29, f32[2,256]{1,0:T(2,128)S(1)} %copy-done.25, ...), channel_id=1, replica_groups=mesh['gx'=4,'gy'=8] {'gx','gy'}, use_global_device_ids=true, to_apply=%region_6.7 | all-reduce | flops 5641 | bytes 45128 | tf_op jit(solution)/shard_map/psum | solution.py:170
  167.1 1.6 copy.28
  169.0 1.4 collective-permute-start.14
  170.4 3.0 %collective-permute-start.15 = (f32[3,2,1,512]{3,2,1,0:T(1,128)S(1)}, f32[3,2,1,512]{3,2,1,0:T(1,128)S(1)}, u32[]{:S(2)}, u32[]{:S(2)}) collective-permute-start(f32[3,2,1,512]{3,2,1,0:T(1,128)S(1)} %get-tuple-element.249), channel_id=1, source_target_pairs={{0,1},{1,2},{2,3},{3,4},{4,5},{5,6},{6,7},{8,9},{9,10},{10,11},{11... | collective-permute-start | bytes 36872 | tf_op jit(solution)/shard_map/ppermute | solution.py:21
  173.5 1.3 collective-permute-start.12
  174.8 4.8 %collective-permute-start.13 = (f32[3,1,16,512]{3,2,1,0:T(8,128)S(1)}, f32[3,1,16,512]{3,2,1,0:T(8,128)S(1)}, u32[]{:S(2)}, u32[]{:S(2)}) collective-permute-start(f32[3,1,16,512]{3,2,1,0:T(8,128)S(1)} %get-tuple-element.247), channel_id=1, source_target_pairs={{0,8},{8,16},{16,24},{1,9},{9,17},{17,25},{2,10},{10,18},{18,26},{... | collective-permute-start | bytes 294920 | tf_op jit(solution)/shard_map/ppermute | solution.py:21
  181.4 2.7 %collective-permute-start.11 = (f32[3,2,1,512]{3,2,1,0:T(1,128)S(1)}, f32[3,2,1,512]{3,2,1,0:T(1,128)S(1)}, u32[]{:S(2)}, u32[]{:S(2)}) collective-permute-start(f32[3,2,1,512]{3,2,1,0:T(1,128)S(1)} %get-tuple-element.253), channel_id=1, source_target_pairs={{0,1},{1,2},{2,3},{3,4},{4,5},{5,6},{6,7},{8,9},{9,10},{10,11},{11... | collective-permute-start | bytes 36872 | tf_op jit(solution)/shard_map/ppermute | solution.py:21
  184.2 1.3 collective-permute-start.8
  185.5 5.2 %collective-permute-start.9 = (f32[3,1,16,512]{3,2,1,0:T(8,128)S(1)}, f32[3,1,16,512]{3,2,1,0:T(8,128)S(1)}, u32[]{:S(2)}, u32[]{:S(2)}) collective-permute-start(f32[3,1,16,512]{3,2,1,0:T(8,128)S(1)} %get-tuple-element.251), channel_id=1, source_target_pairs={{0,8},{8,16},{16,24},{1,9},{9,17},{17,25},{2,10},{10,18},{18,26},{... | collective-permute-start | bytes 294920 | tf_op jit(solution)/shard_map/ppermute | solution.py:21
  190.7 0.9 fusion.49
  192.1 1.8 collective-permute-done.9
  193.9 1.0 fusion.42
  194.8 56.2 %all-reduce.8.cloned.1.call-done = f32[2,256,256]{2,1,0:T(8,128)} async-done(((f32[2,256,256]{2,1,0:T(8,128)}), f32[2,256,256]{2,1,0:T(8,128)}) %all-reduce.8.cloned.1.call-update) | async-done | bytes 524304 | tf_op jit(solution)/shard_map/psum | solution.py:170
  251.0 1.8 multiply_reduce_fusion
  258.3 1.9 broadcast_multiply_fusion.1
  (359 shorter events, 69.2 us)
Async XLA Ops:
  7.2 2.9 %copy-start.13 = (s32[2,16,512]{2,1,0:T(8,128)S(1)}, s32[2,16,512]{2,1,0:T(8,128)}, u32[]{:S(2)}) copy-start(s32[2,16,512]{2,1,0:T(8,128)} %param.15) | copy-start | bytes 196612
  7.2 3.0 %copy-start.20 = (f32[3,2,16,512]{3,2,1,0:T(8,128)S(1)}, f32[3,2,16,512]{3,2,1,0:T(8,128)}, u32[]{:S(2)}) copy-start(f32[3,2,16,512]{3,2,1,0:T(8,128)} %param.20) | copy-start | bytes 589828
  7.2 243.8 %all-reduce.8.cloned.1.call-start = ((), (), s32[]{:S(2)}) async-start(), calls=%async_computation | async-start | bytes 1048576 | tf_op jit(solution)/shard_map/psum | solution.py:170
  8.2 8.4 %copy-start.21 = (f32[3,2,16,512]{3,2,1,0:T(8,128)S(1)}, f32[3,2,16,512]{3,2,1,0:T(8,128)}, u32[]{:S(2)}) copy-start(f32[3,2,16,512]{3,2,1,0:T(8,128)} %param.18) | copy-start | bytes 589828
  9.1 8.3 %copy-start.1 = (f32[3,2,16,512]{3,2,1,0:T(8,128)S(1)}, f32[3,2,16,512]{3,2,1,0:T(8,128)}, u32[]{:S(2)}) copy-start(f32[3,2,16,512]{3,2,1,0:T(8,128)} %param.19) | copy-start | bytes 589828
  10.1 5.0 %copy-start.7 = (f32[1,2,16,512]{3,2,1,0:T(8,128)}, f32[1,2,16,512]{3,2,1,0:T(8,128)S(1)}, u32[]{:S(2)}) copy-start(f32[1,2,16,512]{3,2,1,0:T(8,128)S(1)} %copy.58) | copy-start | bytes 196612
  10.1 19.9 %copy-start.3 = (f32[2,16,512]{2,1,0:T(8,128)}, f32[2,16,512]{2,1,0:T(8,128)S(1)}, u32[]{:S(2)}) copy-start(f32[2,16,512]{2,1,0:T(8,128)S(1)} %get-tuple-element.220) | copy-start | bytes 196612
  10.2 5.0 %copy-start.5 = (f32[2,16,512]{2,1,0:T(8,128)}, f32[2,16,512]{2,1,0:T(8,128)S(1)}, u32[]{:S(2)}) copy-start(f32[2,16,512]{2,1,0:T(8,128)S(1)} %broadcast_select_fusion.1) | copy-start | bytes 196612
  10.2 14.4 %collective-permute-start.1 = (f32[3,1,16,512]{3,2,1,0:T(8,128)S(1)}, f32[3,1,16,512]{3,2,1,0:T(8,128)S(1)}, u32[]{:S(2)}, u32[]{:S(2)}) collective-permute-start(f32[3,1,16,512]{3,2,1,0:T(8,128)S(1)} %get-tuple-element.257), channel_id=1, source_target_pairs={{0,8},{8,16},{16,24},{1,9},{9,17},{17,25},{2,10},{10,18},{18,26},{... | collective-permute-start | bytes 294920 | tf_op jit(solution)/shard_map/ppermute | solution.py:21
  15.1 14.0 %copy-start.26 = (s32[2,16,512]{2,1,0:T(8,128)S(1)}, s32[2,16,512]{2,1,0:T(8,128)}, u32[]{:S(2)}) copy-start(s32[2,16,512]{2,1,0:T(8,128)} %param.16) | copy-start | bytes 196612
  15.1 9.6 %collective-permute-start = (f32[3,1,16,512]{3,2,1,0:T(8,128)S(1)}, f32[3,1,16,512]{3,2,1,0:T(8,128)S(1)}, u32[]{:S(2)}, u32[]{:S(2)}) collective-permute-start(f32[3,1,16,512]{3,2,1,0:T(8,128)S(1)} %get-tuple-element.258), channel_id=1, source_target_pairs={{8,0},{16,8},{24,16},{9,1},{17,9},{25,17},{10,2},{18,10},{26,18},{... | collective-permute-start | bytes 294920 | tf_op jit(solution)/shard_map/ppermute | solution.py:24
  18.2 13.1 %collective-permute-start.5 = (f32[6,1,16,512]{3,2,1,0:T(8,128)}, f32[6,1,16,512]{3,2,1,0:T(8,128)S(1)}, u32[]{:S(2)}, u32[]{:S(2)}) collective-permute-start(f32[6,1,16,512]{3,2,1,0:T(8,128)} %get-tuple-element.240), channel_id=1, source_target_pairs={{0,8},{8,16},{16,24},{1,9},{9,17},{17,25},{2,10},{10,18},{18,26},{... | collective-permute-start | bytes 589832 | tf_op jit(solution)/shard_map/ppermute | solution.py:21
  22.7 10.8 %collective-permute-start.4 = (f32[6,1,16,512]{3,2,1,0:T(8,128)}, f32[6,1,16,512]{3,2,1,0:T(8,128)S(1)}, u32[]{:S(2)}, u32[]{:S(2)}) collective-permute-start(f32[6,1,16,512]{3,2,1,0:T(8,128)} %get-tuple-element.241), channel_id=1, source_target_pairs={{8,0},{16,8},{24,16},{9,1},{17,9},{25,17},{10,2},{18,10},{26,18},{... | collective-permute-start | bytes 589832 | tf_op jit(solution)/shard_map/ppermute | solution.py:24
  24.8 6.0 %collective-permute-start.2 = (f32[3,4,1,512]{3,2,1,0:T(1,128)S(1)}, f32[3,4,1,512]{3,2,1,0:T(1,128)S(1)}, u32[]{:S(2)}, u32[]{:S(2)}) collective-permute-start(f32[3,4,1,512]{3,2,1,0:T(1,128)S(1)} %get-tuple-element.244), channel_id=1, source_target_pairs={{1,0},{2,1},{3,2},{4,3},{5,4},{6,5},{7,6},{9,8},{10,9},{11,10},{12... | collective-permute-start | bytes 73736 | tf_op jit(solution)/shard_map/ppermute | solution.py:24
  26.1 4.7 %collective-permute-start.3 = (f32[3,4,1,512]{3,2,1,0:T(1,128)S(1)}, f32[3,4,1,512]{3,2,1,0:T(1,128)S(1)}, u32[]{:S(2)}, u32[]{:S(2)}) collective-permute-start(f32[3,4,1,512]{3,2,1,0:T(1,128)S(1)} %get-tuple-element.245), channel_id=1, source_target_pairs={{0,1},{1,2},{2,3},{3,4},{4,5},{5,6},{6,7},{8,9},{9,10},{10,11},{11... | collective-permute-start | bytes 73736 | tf_op jit(solution)/shard_map/ppermute | solution.py:21
  33.7 6.0 %copy-start.12 = (bf16[3,1,2,16,512]{4,3,2,0,1:T(8,128)(2,1)S(1)}, bf16[3,1,2,16,512]{4,3,2,0,1:T(8,128)(2,1)}, u32[]{:S(2)}) copy-start(bf16[3,1,2,16,512]{4,3,2,0,1:T(8,128)(2,1)} %get-tuple-element.255) | copy-start | bytes 294916
  33.7 5.4 %collective-permute-start.6 = (f32[6,4,1,512]{3,2,1,0:T(1,128)S(1)}, f32[6,4,1,512]{3,2,1,0:T(1,128)S(1)}, u32[]{:S(2)}, u32[]{:S(2)}) collective-permute-start(f32[6,4,1,512]{3,2,1,0:T(1,128)S(1)} %get-tuple-element.232), channel_id=1, source_target_pairs={{1,0},{2,1},{3,2},{4,3},{5,4},{6,5},{7,6},{9,8},{10,9},{11,10},{12... | collective-permute-start | bytes 147464 | tf_op jit(solution)/shard_map/ppermute | solution.py:24
  35.1 3.9 %collective-permute-start.7 = (f32[6,4,1,512]{3,2,1,0:T(1,128)S(1)}, f32[6,4,1,512]{3,2,1,0:T(1,128)S(1)}, u32[]{:S(2)}, u32[]{:S(2)}) collective-permute-start(f32[6,4,1,512]{3,2,1,0:T(1,128)S(1)} %get-tuple-element.233), channel_id=1, source_target_pairs={{0,1},{1,2},{2,3},{3,4},{4,5},{5,6},{6,7},{8,9},{9,10},{10,11},{11... | collective-permute-start | bytes 147464 | tf_op jit(solution)/shard_map/ppermute | solution.py:21
  40.5 2.7 %copy-start.32 = (bf16[2,256,256]{2,1,0:T(8,128)(2,1)S(1)}, bf16[2,256,256]{2,1,0:T(8,128)(2,1)}, u32[]{:S(2)}) copy-start(bf16[2,256,256]{2,1,0:T(8,128)(2,1)} %get-tuple-element.430) | copy-start | bytes 786436 | tf_op jit(solution)/shard_map/while
  49.4 3.3 %copy-start.32 = (bf16[2,256,256]{2,1,0:T(8,128)(2,1)S(1)}, bf16[2,256,256]{2,1,0:T(8,128)(2,1)}, u32[]{:S(2)}) copy-start(bf16[2,256,256]{2,1,0:T(8,128)(2,1)} %get-tuple-element.430) | copy-start | bytes 786436 | tf_op jit(solution)/shard_map/while
  56.2 1.1 copy-start.24
  59.0 3.3 %copy-start.32 = (bf16[2,256,256]{2,1,0:T(8,128)(2,1)S(1)}, bf16[2,256,256]{2,1,0:T(8,128)(2,1)}, u32[]{:S(2)}) copy-start(bf16[2,256,256]{2,1,0:T(8,128)(2,1)} %get-tuple-element.430) | copy-start | bytes 786436 | tf_op jit(solution)/shard_map/while
  68.6 3.3 %copy-start.32 = (bf16[2,256,256]{2,1,0:T(8,128)(2,1)S(1)}, bf16[2,256,256]{2,1,0:T(8,128)(2,1)}, u32[]{:S(2)}) copy-start(bf16[2,256,256]{2,1,0:T(8,128)(2,1)} %get-tuple-element.430) | copy-start | bytes 786436 | tf_op jit(solution)/shard_map/while
  75.4 1.1 copy-start.24
  78.2 3.3 %copy-start.32 = (bf16[2,256,256]{2,1,0:T(8,128)(2,1)S(1)}, bf16[2,256,256]{2,1,0:T(8,128)(2,1)}, u32[]{:S(2)}) copy-start(bf16[2,256,256]{2,1,0:T(8,128)(2,1)} %get-tuple-element.430) | copy-start | bytes 786436 | tf_op jit(solution)/shard_map/while
  85.0 1.1 copy-start.24
  87.8 3.4 %copy-start.32 = (bf16[2,256,256]{2,1,0:T(8,128)(2,1)S(1)}, bf16[2,256,256]{2,1,0:T(8,128)(2,1)}, u32[]{:S(2)}) copy-start(bf16[2,256,256]{2,1,0:T(8,128)(2,1)} %get-tuple-element.430) | copy-start | bytes 786436 | tf_op jit(solution)/shard_map/while
  97.3 3.3 %copy-start.32 = (bf16[2,256,256]{2,1,0:T(8,128)(2,1)S(1)}, bf16[2,256,256]{2,1,0:T(8,128)(2,1)}, u32[]{:S(2)}) copy-start(bf16[2,256,256]{2,1,0:T(8,128)(2,1)} %get-tuple-element.430) | copy-start | bytes 786436 | tf_op jit(solution)/shard_map/while
  106.9 3.4 %copy-start.32 = (bf16[2,256,256]{2,1,0:T(8,128)(2,1)S(1)}, bf16[2,256,256]{2,1,0:T(8,128)(2,1)}, u32[]{:S(2)}) copy-start(bf16[2,256,256]{2,1,0:T(8,128)(2,1)} %get-tuple-element.430) | copy-start | bytes 786436 | tf_op jit(solution)/shard_map/while
  113.7 1.1 copy-start.24
  116.5 1.1 copy-start
  118.4 1.5 copy-start.11
  118.4 1.5 copy-start.25
  118.4 1.5 copy-start.29
  118.4 1.5 copy-start.30
  118.5 73.0 %collective-permute-start.10 = (f32[3,2,1,512]{3,2,1,0:T(1,128)S(1)}, f32[3,2,1,512]{3,2,1,0:T(1,128)S(1)}, u32[]{:S(2)}, u32[]{:S(2)}) collective-permute-start(f32[3,2,1,512]{3,2,1,0:T(1,128)S(1)} %get-tuple-element.252), channel_id=1, source_target_pairs={{1,0},{2,1},{3,2},{4,3},{5,4},{6,5},{7,6},{9,8},{10,9},{11,10},{12... | collective-permute-start | bytes 36872 | tf_op jit(solution)/shard_map/ppermute | solution.py:24
  168.8 25.0 %copy-start.2 = (f32[3,2,16,512]{3,2,1,0:T(8,128)S(1)}, f32[3,2,16,512]{3,2,1,0:T(8,128)}, u32[]{:S(2)}) copy-start(f32[3,2,16,512]{3,2,1,0:T(8,128)} %param.19) | copy-start | bytes 589828
  168.8 25.0 %copy-start.6 = (f32[2,16,512]{2,1,0:T(8,128)S(1)}, f32[2,16,512]{2,1,0:T(8,128)}, u32[]{:S(2)}) copy-start(f32[2,16,512]{2,1,0:T(8,128)} %copy-done.5) | copy-start | bytes 196612
  168.8 25.0 %copy-start.8 = (f32[1,2,16,512]{3,2,1,0:T(8,128)S(1)}, f32[1,2,16,512]{3,2,1,0:T(8,128)}, u32[]{:S(2)}) copy-start(f32[1,2,16,512]{3,2,1,0:T(8,128)} %copy-done.7) | copy-start | bytes 196612
  168.9 25.0 %copy-start.17 = (f32[6,4,1,512]{3,2,1,0:T(1,128)S(1)}, f32[6,4,1,512]{3,2,1,0:T(1,128)}, u32[]{:S(2)}) copy-start(f32[6,4,1,512]{3,2,1,0:T(1,128)} %copy-done.16) | copy-start | bytes 147460
  168.9 25.0 %copy-start.19 = (f32[6,4,1,512]{3,2,1,0:T(1,128)S(1)}, f32[6,4,1,512]{3,2,1,0:T(1,128)}, u32[]{:S(2)}) copy-start(f32[6,4,1,512]{3,2,1,0:T(1,128)} %copy-done.18) | copy-start | bytes 147460
  169.0 12.5 %collective-permute-start.14 = (f32[3,2,1,512]{3,2,1,0:T(1,128)S(1)}, f32[3,2,1,512]{3,2,1,0:T(1,128)S(1)}, u32[]{:S(2)}, u32[]{:S(2)}) collective-permute-start(f32[3,2,1,512]{3,2,1,0:T(1,128)S(1)} %get-tuple-element.248), channel_id=1, source_target_pairs={{1,0},{2,1},{3,2},{4,3},{5,4},{6,5},{7,6},{9,8},{10,9},{11,10},{12... | collective-permute-start | bytes 36872 | tf_op jit(solution)/shard_map/ppermute | solution.py:24
  170.4 13.8 %collective-permute-start.15 = (f32[3,2,1,512]{3,2,1,0:T(1,128)S(1)}, f32[3,2,1,512]{3,2,1,0:T(1,128)S(1)}, u32[]{:S(2)}, u32[]{:S(2)}) collective-permute-start(f32[3,2,1,512]{3,2,1,0:T(1,128)S(1)} %get-tuple-element.249), channel_id=1, source_target_pairs={{0,1},{1,2},{2,3},{3,4},{4,5},{5,6},{6,7},{8,9},{9,10},{10,11},{11... | collective-permute-start | bytes 36872 | tf_op jit(solution)/shard_map/ppermute | solution.py:21
  173.5 12.1 %collective-permute-start.12 = (f32[3,1,16,512]{3,2,1,0:T(8,128)S(1)}, f32[3,1,16,512]{3,2,1,0:T(8,128)S(1)}, u32[]{:S(2)}, u32[]{:S(2)}) collective-permute-start(f32[3,1,16,512]{3,2,1,0:T(8,128)S(1)} %get-tuple-element.246), channel_id=1, source_target_pairs={{8,0},{16,8},{24,16},{9,1},{17,9},{25,17},{10,2},{18,10},{26,18},{... | collective-permute-start | bytes 294920 | tf_op jit(solution)/shard_map/ppermute | solution.py:24
  174.8 15.9 %collective-permute-start.13 = (f32[3,1,16,512]{3,2,1,0:T(8,128)S(1)}, f32[3,1,16,512]{3,2,1,0:T(8,128)S(1)}, u32[]{:S(2)}, u32[]{:S(2)}) collective-permute-start(f32[3,1,16,512]{3,2,1,0:T(8,128)S(1)} %get-tuple-element.247), channel_id=1, source_target_pairs={{0,8},{8,16},{16,24},{1,9},{9,17},{17,25},{2,10},{10,18},{18,26},{... | collective-permute-start | bytes 294920 | tf_op jit(solution)/shard_map/ppermute | solution.py:21
  181.4 10.1 %collective-permute-start.11 = (f32[3,2,1,512]{3,2,1,0:T(1,128)S(1)}, f32[3,2,1,512]{3,2,1,0:T(1,128)S(1)}, u32[]{:S(2)}, u32[]{:S(2)}) collective-permute-start(f32[3,2,1,512]{3,2,1,0:T(1,128)S(1)} %get-tuple-element.253), channel_id=1, source_target_pairs={{0,1},{1,2},{2,3},{3,4},{4,5},{5,6},{6,7},{8,9},{9,10},{10,11},{11... | collective-permute-start | bytes 36872 | tf_op jit(solution)/shard_map/ppermute | solution.py:21
  184.2 7.9 %collective-permute-start.8 = (f32[3,1,16,512]{3,2,1,0:T(8,128)S(1)}, f32[3,1,16,512]{3,2,1,0:T(8,128)S(1)}, u32[]{:S(2)}, u32[]{:S(2)}) collective-permute-start(f32[3,1,16,512]{3,2,1,0:T(8,128)S(1)} %get-tuple-element.250), channel_id=1, source_target_pairs={{8,0},{16,8},{24,16},{9,1},{17,9},{25,17},{10,2},{18,10},{26,18},{... | collective-permute-start | bytes 294920 | tf_op jit(solution)/shard_map/ppermute | solution.py:24
  185.5 8.3 %collective-permute-start.9 = (f32[3,1,16,512]{3,2,1,0:T(8,128)S(1)}, f32[3,1,16,512]{3,2,1,0:T(8,128)S(1)}, u32[]{:S(2)}, u32[]{:S(2)}) collective-permute-start(f32[3,1,16,512]{3,2,1,0:T(8,128)S(1)} %get-tuple-element.251), channel_id=1, source_target_pairs={{0,8},{8,16},{16,24},{1,9},{9,17},{17,25},{2,10},{10,18},{18,26},{... | collective-permute-start | bytes 294920 | tf_op jit(solution)/shard_map/ppermute | solution.py:21
  (44 other events, 30.7 us)
Sparse Core Ops, SparseCore 0:
  118.6 132.3 all-reduce.7
where the time goes:
time: 269 us; the launch traced here: 267 us
  waiting for transfers between devices  60.7 us (23%)
  matrix products  50.9 us (19%)
  blocking collectives  44.8 us (17%)
  starting transfers between devices  41.9 us (16%)
  other arithmetic  26.1 us (10%)
  local copies, waits for them, and re-layouts  22.3 us (8%)
  between operations  19.4 us (7%)
    psum x1, waiting for transfers between devices, body(): lax.psum((partials[0], partials[1], partials[2], partials[3], partials[4]...  56.2 us
    psum x1, blocking collectives, body(): lax.psum((partials[0], partials[1], partials[2], partials[3], partials[4]...  44.8 us
    ppermute x8, starting transfers between devices, with_halo(): lax.ppermute(lax.slice_in_dim(block, block.shape[dim] - width, None, axis...  31.2 us
    ppermute x8, starting transfers between devices, with_halo(): lax.ppermute(lax.slice_in_dim(block, 0, width, axis=dim), axis, backward)  10.7 us
    add x32, other arithmetic, backward_step(): left + right  10.1 us
    dot_general x8, matrix products, forward_block(): jnp.dot(w_in, feats, preferred_element_type=jnp.float32) + b_in[:, None]  9.4 us
    slice x8, local copies, waits for them, and re-layouts, forward_block(): b_mid[1][:, None]  6.08 us
    dynamic_update_slice x8, local copies, waits for them, and re-layouts, body(): lax.scan(backward_step, zeros, (feat_blocks, delta_all))  5.41 us
  transfers between devices with their start and end apart: 17, of which 4 were waited for; matrix products, arithmetic and copies ran while one was open for 4% of the time, Pallas kernels for 0%

commit v1 on v0

--- a/solution.py
+++ b/solution.py
@@ -168,7 +168,10 @@
         + zdiff(strain_grad[:, 2])
     )
     summed = lax.psum(
-        (partials[0], partials[1], partials[2], partials[3], partials[4], partials[5]), ("gx", "gy")
+        lax.psum(
+            (partials[0], partials[1], partials[2], partials[3], partials[4], partials[5]), "gy"
+        ),
+        "gx",
     )
     total = sum((jnp.sum(jnp.square(item)) for item in summed))
     scale = lax.rsqrt(total / NPARAM + norm_eps)

time: 269 us -> 247 us (0.918)
  waiting for transfers between devices: 60.7 us -> 35.6 us
  blocking collectives: 44.8 us -> 50.1 us
    psum x1, waiting for transfers between devices: 56.2 us -> 0.02 us  [body(): lax.psum((partials[0], partials[1], partials[2], partials[3], partials[4]...]
    psum x0 -> x1, waiting for transfers between devices: none -> 31.9 us  [body(): lax.psum(lax.psum((partials[0], partials[1], partials[2], partials[3], pa...]
    psum x0 -> x1, blocking collectives: none -> 17.2 us  [body(): lax.psum(lax.psum((partials[0], partials[1], partials[2], partials[3], pa...]
    psum x1, blocking collectives: 44.8 us -> 33 us  [body(): lax.psum((partials[0], partials[1], partials[2], partials[3], partials[4]...]
  transfers between devices with their start and end apart: 17 -> 18, of which waited for: 4 -> 3; matrix products, arithmetic and copies ran while one was open for 4% -> 5% of each run, Pallas kernels for 0% -> 0%
where the time goes in v1:
time: 247 us; the launch traced here: 245 us
  matrix products  50.9 us (21%)
  blocking collectives  50.1 us (20%)
  starting transfers between devices  39.8 us (16%)
  waiting for transfers between devices  35.6 us (14%)
  other arithmetic  26.1 us (11%)
  local copies, waits for them, and re-layouts  22.3 us (9%)
  between operations  19.4 us (8%)
    psum x1, blocking collectives, body(): lax.psum((partials[0], partials[1], partials[2], partials[3], partials[4]...  33 us
    psum x1, waiting for transfers between devices, body(): lax.psum(lax.psum((partials[0], partials[1], partials[2], partials[3], pa...  31.9 us
    ppermute x8, starting transfers between devices, with_halo(): lax.ppermute(lax.slice_in_dim(block, block.shape[dim] - width, None, axis...  29 us
    psum x1, blocking collectives, body(): lax.psum(lax.psum((partials[0], partials[1], partials[2], partials[3], pa...  17.2 us
    ppermute x8, starting transfers between devices, with_halo(): lax.ppermute(lax.slice_in_dim(block, 0, width, axis=dim), axis, backward)  10.7 us
    add x32, other arithmetic, backward_step(): left + right  10.1 us
    dot_general x8, matrix products, forward_block(): jnp.dot(w_in, feats, preferred_element_type=jnp.float32) + b_in[:, None]  9.41 us
    slice x8, local copies, waits for them, and re-layouts, forward_block(): b_mid[1][:, None]  6.08 us
  transfers between devices with their start and end apart: 18, of which 3 were waited for; matrix products, arithmetic and copies ran while one was open for 5% of the time, Pallas kernels for 0%

profile of v1, /device:TPU:0, one launch (start us, length us, event | category | flops | bytes accessed | tf_op | source)
XLA Modules:
  0.0 245.0 jit_solution(13181759675077743735)
XLA Ops:
  7.2 0.9 iota_compare_fusion
  8.2 0.9 fusion.70
  9.1 0.9 fusion.72
  10.2 4.8 %collective-permute-start.1 = (f32[3,1,16,512]{3,2,1,0:T(8,128)S(1)}, f32[3,1,16,512]{3,2,1,0:T(8,128)S(1)}, u32[]{:S(2)}, u32[]{:S(2)}) collective-permute-start(f32[3,1,16,512]{3,2,1,0:T(8,128)S(1)} %get-tuple-element.262), channel_id=1, source_target_pairs={{0,8},{8,16},{16,24},{1,9},{9,17},{17,25},{2,10},{10,18},{18,26},{... | collective-permute-start | bytes 294920 | tf_op jit(solution)/shard_map/ppermute | solution.py:21
  15.1 1.4 collective-permute-start
  16.6 0.8 constant_dynamic-update-slice_fusion.1
  17.4 0.8 fusion.78
  18.2 4.5 %collective-permute-start.5 = (f32[6,1,16,512]{3,2,1,0:T(8,128)}, f32[6,1,16,512]{3,2,1,0:T(8,128)S(1)}, u32[]{:S(2)}, u32[]{:S(2)}) collective-permute-start(f32[6,1,16,512]{3,2,1,0:T(8,128)} %get-tuple-element.245), channel_id=1, source_target_pairs={{0,8},{8,16},{16,24},{1,9},{9,17},{17,25},{2,10},{10,18},{18,26},{... | collective-permute-start | bytes 589832 | tf_op jit(solution)/shard_map/ppermute | solution.py:21
  22.7 1.3 collective-permute-start.4
  24.8 1.3 collective-permute-start.2
  26.1 3.0 %collective-permute-start.3 = (f32[3,4,1,512]{3,2,1,0:T(1,128)S(1)}, f32[3,4,1,512]{3,2,1,0:T(1,128)S(1)}, u32[]{:S(2)}, u32[]{:S(2)}) collective-permute-start(f32[3,4,1,512]{3,2,1,0:T(1,128)S(1)} %get-tuple-element.250), channel_id=1, source_target_pairs={{0,1},{1,2},{2,3},{3,4},{4,5},{5,6},{6,7},{8,9},{9,10},{10,11},{11... | collective-permute-start | bytes 73736 | tf_op jit(solution)/shard_map/ppermute | solution.py:21
  31.3 2.3 collective-permute-done.4
  33.7 1.4 collective-permute-start.6
  35.1 3.0 %collective-permute-start.7 = (f32[6,4,1,512]{3,2,1,0:T(1,128)S(1)}, f32[6,4,1,512]{3,2,1,0:T(1,128)S(1)}, u32[]{:S(2)}, u32[]{:S(2)}) collective-permute-start(f32[6,4,1,512]{3,2,1,0:T(1,128)S(1)} %get-tuple-element.238), channel_id=1, source_target_pairs={{0,1},{1,2},{2,3},{3,4},{4,5},{5,6},{6,7},{8,9},{9,10},{10,11},{11... | collective-permute-start | bytes 147464 | tf_op jit(solution)/shard_map/ppermute | solution.py:21
  38.1 0.9 multiply_bitcast_fusion
  40.5 76.0 %while.25 = (s32[]{:T(128)}, f32[256,10]{0,1:T(8,128)S(1)}, f32[256]{0:T(256)}, f32[2,256,256]{2,1,0:T(8,128)S(1)}, f32[2,256]{1,0:T(2,128)}, /*index=5*/f32[9,2...) while((s32[]{:T(128)}, f32[256,10]{0,1:T(8,128)S(1)}, ...), condition=%wide.region_5.6_spmd.clone, body=%wide.region_0.5_spmd.clone.sunk | while | flops 1684996864 | bytes 26539676 | solution.py:145
  42.0 1.2 fusion.149
  50.4 1.2 fusion.153
  51.6 1.2 fusion.149
  60.0 1.2 fusion.153
  61.2 1.2 fusion.149
  69.6 1.2 fusion.153
  70.7 1.2 fusion.149
  79.2 1.2 fusion.153
  80.3 1.2 fusion.149
  88.8 1.2 fusion.153
  89.9 1.2 fusion.149
  98.3 1.2 fusion.153
  99.5 1.2 fusion.149
  107.9 1.2 fusion.153
  109.1 1.2 fusion.149
  118.6 1.3 collective-permute-start.10
  119.9 33.0 %all-reduce.5 = (f32[256,10]{0,1:T(8,128)S(1)}, f32[256]{0:T(256)S(1)}, f32[2,256]{1,0:T(2,128)S(1)}, f32[9,256]{1,0:T(8,128)S(1)}, f32[9]{0:T(128)S(1)}) all-reduce(f32[256,10]{0,1:T(8,128)S(1)} %copy-done.11, f32[256]{0:T(256)S(1)} %copy-done.29, f32[2,256]{1,0:T(2,128)S(1)} %copy-done.25, ...), channel_id=1, replica_groups=mesh['gx'=4,'gy'=8] {'gy'}, use_global_device_ids=true, to_apply=%region_6.7 | all-reduce | flops 5641 | bytes 45128 | tf_op jit(solution)/shard_map/psum | solution.py:171
  152.9 17.2 %all-reduce.6 = (f32[256,10]{0,1:T(8,128)S(1)}, f32[256]{0:T(256)S(1)}, f32[2,256]{1,0:T(2,128)S(1)}, f32[9,256]{1,0:T(8,128)S(1)}, f32[9]{0:T(128)S(1)}) all-reduce(f32[256,10]{0,1:T(8,128)S(1)} %get-tuple-element.215, f32[256]{0:T(256)S(1)} %get-tuple-element.216, ...), channel_id=1, replica_groups=mesh['gx'=4,'gy'=8] {'gx'}, use_global_device_ids=true, to_apply=%region_7.8 | all-reduce | flops 5641 | bytes 45128 | tf_op jit(solution)/shard_map/psum | solution.py:170
  171.9 1.6 copy.28
  173.7 1.3 collective-permute-start.14
  175.0 3.0 %collective-permute-start.15 = (f32[3,2,1,512]{3,2,1,0:T(1,128)S(1)}, f32[3,2,1,512]{3,2,1,0:T(1,128)S(1)}, u32[]{:S(2)}, u32[]{:S(2)}) collective-permute-start(f32[3,2,1,512]{3,2,1,0:T(1,128)S(1)} %get-tuple-element.254), channel_id=1, source_target_pairs={{0,1},{1,2},{2,3},{3,4},{4,5},{5,6},{6,7},{8,9},{9,10},{10,11},{11... | collective-permute-start | bytes 36872 | tf_op jit(solution)/shard_map/ppermute | solution.py:21
  178.1 1.4 collective-permute-start.12
  179.5 4.6 %collective-permute-start.13 = (f32[3,1,16,512]{3,2,1,0:T(8,128)S(1)}, f32[3,1,16,512]{3,2,1,0:T(8,128)S(1)}, u32[]{:S(2)}, u32[]{:S(2)}) collective-permute-start(f32[3,1,16,512]{3,2,1,0:T(8,128)S(1)} %get-tuple-element.252), channel_id=1, source_target_pairs={{0,8},{8,16},{16,24},{1,9},{9,17},{17,25},{2,10},{10,18},{18,26},{... | collective-permute-start | bytes 294920 | tf_op jit(solution)/shard_map/ppermute | solution.py:21
  186.7 1.4 collective-permute-start.11
  188.1 1.3 collective-permute-start.8
  189.4 4.6 %collective-permute-start.9 = (f32[3,1,16,512]{3,2,1,0:T(8,128)S(1)}, f32[3,1,16,512]{3,2,1,0:T(8,128)S(1)}, u32[]{:S(2)}, u32[]{:S(2)}) collective-permute-start(f32[3,1,16,512]{3,2,1,0:T(8,128)S(1)} %get-tuple-element.256), channel_id=1, source_target_pairs={{0,8},{8,16},{16,24},{1,9},{9,17},{17,25},{2,10},{10,18},{18,26},{... | collective-permute-start | bytes 294920 | tf_op jit(solution)/shard_map/ppermute | solution.py:21
  193.9 0.9 fusion.49
  194.8 1.3 collective-permute-done.9
  196.2 1.0 fusion.42
  197.1 31.9 %all-reduce.12.cloned.1.call-done = f32[2,256,256]{2,1,0:T(8,128)} async-done(((f32[2,256,256]{2,1,0:T(8,128)}), f32[2,256,256]{2,1,0:T(8,128)}) %all-reduce.12.cloned.1.call-update) | async-done | bytes 524304 | tf_op jit(solution)/shard_map/psum | solution.py:170
  229.0 1.8 multiply_reduce_fusion
  236.3 1.9 broadcast_multiply_fusion.1
  (363 shorter events, 69.6 us)
Async XLA Ops:
  7.2 2.9 %copy-start.13 = (s32[2,16,512]{2,1,0:T(8,128)S(1)}, s32[2,16,512]{2,1,0:T(8,128)}, u32[]{:S(2)}) copy-start(s32[2,16,512]{2,1,0:T(8,128)} %param.15) | copy-start | bytes 196612
  7.2 3.0 %copy-start.20 = (f32[3,2,16,512]{3,2,1,0:T(8,128)S(1)}, f32[3,2,16,512]{3,2,1,0:T(8,128)}, u32[]{:S(2)}) copy-start(f32[3,2,16,512]{3,2,1,0:T(8,128)} %param.20) | copy-start | bytes 589828
  7.2 177.0 %all-reduce.10.cloned.1.call-start = ((), (), s32[]{:S(2)}) async-start(), calls=%async_computation | async-start | bytes 1048576 | tf_op jit(solution)/shard_map/psum | solution.py:171
  8.2 8.4 %copy-start.21 = (f32[3,2,16,512]{3,2,1,0:T(8,128)S(1)}, f32[3,2,16,512]{3,2,1,0:T(8,128)}, u32[]{:S(2)}) copy-start(f32[3,2,16,512]{3,2,1,0:T(8,128)} %param.18) | copy-start | bytes 589828
  9.1 8.3 %copy-start.1 = (f32[3,2,16,512]{3,2,1,0:T(8,128)S(1)}, f32[3,2,16,512]{3,2,1,0:T(8,128)}, u32[]{:S(2)}) copy-start(f32[3,2,16,512]{3,2,1,0:T(8,128)} %param.19) | copy-start | bytes 589828
  10.1 5.0 %copy-start.7 = (f32[1,2,16,512]{3,2,1,0:T(8,128)}, f32[1,2,16,512]{3,2,1,0:T(8,128)S(1)}, u32[]{:S(2)}) copy-start(f32[1,2,16,512]{3,2,1,0:T(8,128)S(1)} %copy.58) | copy-start | bytes 196612
  10.1 19.9 %copy-start.3 = (f32[2,16,512]{2,1,0:T(8,128)}, f32[2,16,512]{2,1,0:T(8,128)S(1)}, u32[]{:S(2)}) copy-start(f32[2,16,512]{2,1,0:T(8,128)S(1)} %get-tuple-element.225) | copy-start | bytes 196612
  10.2 5.0 %copy-start.5 = (f32[2,16,512]{2,1,0:T(8,128)}, f32[2,16,512]{2,1,0:T(8,128)S(1)}, u32[]{:S(2)}) copy-start(f32[2,16,512]{2,1,0:T(8,128)S(1)} %broadcast_select_fusion.1) | copy-start | bytes 196612
  10.2 14.4 %collective-permute-start.1 = (f32[3,1,16,512]{3,2,1,0:T(8,128)S(1)}, f32[3,1,16,512]{3,2,1,0:T(8,128)S(1)}, u32[]{:S(2)}, u32[]{:S(2)}) collective-permute-start(f32[3,1,16,512]{3,2,1,0:T(8,128)S(1)} %get-tuple-element.262), channel_id=1, source_target_pairs={{0,8},{8,16},{16,24},{1,9},{9,17},{17,25},{2,10},{10,18},{18,26},{... | collective-permute-start | bytes 294920 | tf_op jit(solution)/shard_map/ppermute | solution.py:21
  15.1 14.0 %copy-start.26 = (s32[2,16,512]{2,1,0:T(8,128)S(1)}, s32[2,16,512]{2,1,0:T(8,128)}, u32[]{:S(2)}) copy-start(s32[2,16,512]{2,1,0:T(8,128)} %param.16) | copy-start | bytes 196612
  15.1 9.6 %collective-permute-start = (f32[3,1,16,512]{3,2,1,0:T(8,128)S(1)}, f32[3,1,16,512]{3,2,1,0:T(8,128)S(1)}, u32[]{:S(2)}, u32[]{:S(2)}) collective-permute-start(f32[3,1,16,512]{3,2,1,0:T(8,128)S(1)} %get-tuple-element.263), channel_id=1, source_target_pairs={{8,0},{16,8},{24,16},{9,1},{17,9},{25,17},{10,2},{18,10},{26,18},{... | collective-permute-start | bytes 294920 | tf_op jit(solution)/shard_map/ppermute | solution.py:24
  18.2 13.1 %collective-permute-start.5 = (f32[6,1,16,512]{3,2,1,0:T(8,128)}, f32[6,1,16,512]{3,2,1,0:T(8,128)S(1)}, u32[]{:S(2)}, u32[]{:S(2)}) collective-permute-start(f32[6,1,16,512]{3,2,1,0:T(8,128)} %get-tuple-element.245), channel_id=1, source_target_pairs={{0,8},{8,16},{16,24},{1,9},{9,17},{17,25},{2,10},{10,18},{18,26},{... | collective-permute-start | bytes 589832 | tf_op jit(solution)/shard_map/ppermute | solution.py:21
  22.7 10.8 %collective-permute-start.4 = (f32[6,1,16,512]{3,2,1,0:T(8,128)}, f32[6,1,16,512]{3,2,1,0:T(8,128)S(1)}, u32[]{:S(2)}, u32[]{:S(2)}) collective-permute-start(f32[6,1,16,512]{3,2,1,0:T(8,128)} %get-tuple-element.246), channel_id=1, source_target_pairs={{8,0},{16,8},{24,16},{9,1},{17,9},{25,17},{10,2},{18,10},{26,18},{... | collective-permute-start | bytes 589832 | tf_op jit(solution)/shard_map/ppermute | solution.py:24
  24.8 6.0 %collective-permute-start.2 = (f32[3,4,1,512]{3,2,1,0:T(1,128)S(1)}, f32[3,4,1,512]{3,2,1,0:T(1,128)S(1)}, u32[]{:S(2)}, u32[]{:S(2)}) collective-permute-start(f32[3,4,1,512]{3,2,1,0:T(1,128)S(1)} %get-tuple-element.249), channel_id=1, source_target_pairs={{1,0},{2,1},{3,2},{4,3},{5,4},{6,5},{7,6},{9,8},{10,9},{11,10},{12... | collective-permute-start | bytes 73736 | tf_op jit(solution)/shard_map/ppermute | solution.py:24
  26.1 4.7 %collective-permute-start.3 = (f32[3,4,1,512]{3,2,1,0:T(1,128)S(1)}, f32[3,4,1,512]{3,2,1,0:T(1,128)S(1)}, u32[]{:S(2)}, u32[]{:S(2)}) collective-permute-start(f32[3,4,1,512]{3,2,1,0:T(1,128)S(1)} %get-tuple-element.250), channel_id=1, source_target_pairs={{0,1},{1,2},{2,3},{3,4},{4,5},{5,6},{6,7},{8,9},{9,10},{10,11},{11... | collective-permute-start | bytes 73736 | tf_op jit(solution)/shard_map/ppermute | solution.py:21
  33.7 6.0 %copy-start.12 = (bf16[3,1,2,16,512]{4,3,2,0,1:T(8,128)(2,1)S(1)}, bf16[3,1,2,16,512]{4,3,2,0,1:T(8,128)(2,1)}, u32[]{:S(2)}) copy-start(bf16[3,1,2,16,512]{4,3,2,0,1:T(8,128)(2,1)} %get-tuple-element.260) | copy-start | bytes 294916
  33.7 5.4 %collective-permute-start.6 = (f32[6,4,1,512]{3,2,1,0:T(1,128)S(1)}, f32[6,4,1,512]{3,2,1,0:T(1,128)S(1)}, u32[]{:S(2)}, u32[]{:S(2)}) collective-permute-start(f32[6,4,1,512]{3,2,1,0:T(1,128)S(1)} %get-tuple-element.237), channel_id=1, source_target_pairs={{1,0},{2,1},{3,2},{4,3},{5,4},{6,5},{7,6},{9,8},{10,9},{11,10},{12... | collective-permute-start | bytes 147464 | tf_op jit(solution)/shard_map/ppermute | solution.py:24
  35.1 3.9 %collective-permute-start.7 = (f32[6,4,1,512]{3,2,1,0:T(1,128)S(1)}, f32[6,4,1,512]{3,2,1,0:T(1,128)S(1)}, u32[]{:S(2)}, u32[]{:S(2)}) collective-permute-start(f32[6,4,1,512]{3,2,1,0:T(1,128)S(1)} %get-tuple-element.238), channel_id=1, source_target_pairs={{0,1},{1,2},{2,3},{3,4},{4,5},{5,6},{6,7},{8,9},{9,10},{10,11},{11... | collective-permute-start | bytes 147464 | tf_op jit(solution)/shard_map/ppermute | solution.py:21
  40.5 2.7 %copy-start.32 = (bf16[2,256,256]{2,1,0:T(8,128)(2,1)S(1)}, bf16[2,256,256]{2,1,0:T(8,128)(2,1)}, u32[]{:S(2)}) copy-start(bf16[2,256,256]{2,1,0:T(8,128)(2,1)} %get-tuple-element.435) | copy-start | bytes 786436 | tf_op jit(solution)/shard_map/while
  49.4 3.4 %copy-start.32 = (bf16[2,256,256]{2,1,0:T(8,128)(2,1)S(1)}, bf16[2,256,256]{2,1,0:T(8,128)(2,1)}, u32[]{:S(2)}) copy-start(bf16[2,256,256]{2,1,0:T(8,128)(2,1)} %get-tuple-element.435) | copy-start | bytes 786436 | tf_op jit(solution)/shard_map/while
  59.0 3.3 %copy-start.32 = (bf16[2,256,256]{2,1,0:T(8,128)(2,1)S(1)}, bf16[2,256,256]{2,1,0:T(8,128)(2,1)}, u32[]{:S(2)}) copy-start(bf16[2,256,256]{2,1,0:T(8,128)(2,1)} %get-tuple-element.435) | copy-start | bytes 786436 | tf_op jit(solution)/shard_map/while
  65.8 1.1 copy-start.24
  68.6 3.4 %copy-start.32 = (bf16[2,256,256]{2,1,0:T(8,128)(2,1)S(1)}, bf16[2,256,256]{2,1,0:T(8,128)(2,1)}, u32[]{:S(2)}) copy-start(bf16[2,256,256]{2,1,0:T(8,128)(2,1)} %get-tuple-element.435) | copy-start | bytes 786436 | tf_op jit(solution)/shard_map/while
  75.4 1.1 copy-start.24
  78.2 3.3 %copy-start.32 = (bf16[2,256,256]{2,1,0:T(8,128)(2,1)S(1)}, bf16[2,256,256]{2,1,0:T(8,128)(2,1)}, u32[]{:S(2)}) copy-start(bf16[2,256,256]{2,1,0:T(8,128)(2,1)} %get-tuple-element.435) | copy-start | bytes 786436 | tf_op jit(solution)/shard_map/while
  87.8 3.3 %copy-start.32 = (bf16[2,256,256]{2,1,0:T(8,128)(2,1)S(1)}, bf16[2,256,256]{2,1,0:T(8,128)(2,1)}, u32[]{:S(2)}) copy-start(bf16[2,256,256]{2,1,0:T(8,128)(2,1)} %get-tuple-element.435) | copy-start | bytes 786436 | tf_op jit(solution)/shard_map/while
  94.6 1.1 copy-start.24
  97.4 3.3 %copy-start.32 = (bf16[2,256,256]{2,1,0:T(8,128)(2,1)S(1)}, bf16[2,256,256]{2,1,0:T(8,128)(2,1)}, u32[]{:S(2)}) copy-start(bf16[2,256,256]{2,1,0:T(8,128)(2,1)} %get-tuple-element.435) | copy-start | bytes 786436 | tf_op jit(solution)/shard_map/while
  106.9 3.3 %copy-start.32 = (bf16[2,256,256]{2,1,0:T(8,128)(2,1)S(1)}, bf16[2,256,256]{2,1,0:T(8,128)(2,1)}, u32[]{:S(2)}) copy-start(bf16[2,256,256]{2,1,0:T(8,128)(2,1)} %get-tuple-element.435) | copy-start | bytes 786436 | tf_op jit(solution)/shard_map/while
  116.5 1.1 copy-start
  118.4 1.5 copy-start.11
  118.4 1.5 copy-start.25
  118.4 1.5 copy-start.29
  118.4 1.5 copy-start.30
  118.5 110.5 %all-reduce.12.cloned.1.call-start = ((), (), s32[]{:S(2)}) async-start(), calls=%async_computation.1 | async-start | bytes 1048576 | tf_op jit(solution)/shard_map/psum | solution.py:170
  118.6 76.2 %collective-permute-start.10 = (f32[3,2,1,512]{3,2,1,0:T(1,128)S(1)}, f32[3,2,1,512]{3,2,1,0:T(1,128)S(1)}, u32[]{:S(2)}, u32[]{:S(2)}) collective-permute-start(f32[3,2,1,512]{3,2,1,0:T(1,128)S(1)} %get-tuple-element.257), channel_id=1, source_target_pairs={{1,0},{2,1},{3,2},{4,3},{5,4},{6,5},{7,6},{9,8},{10,9},{11,10},{12... | collective-permute-start | bytes 36872 | tf_op jit(solution)/shard_map/ppermute | solution.py:24
  173.7 13.0 %collective-permute-start.14 = (f32[3,2,1,512]{3,2,1,0:T(1,128)S(1)}, f32[3,2,1,512]{3,2,1,0:T(1,128)S(1)}, u32[]{:S(2)}, u32[]{:S(2)}) collective-permute-start(f32[3,2,1,512]{3,2,1,0:T(1,128)S(1)} %get-tuple-element.253), channel_id=1, source_target_pairs={{1,0},{2,1},{3,2},{4,3},{5,4},{6,5},{7,6},{9,8},{10,9},{11,10},{12... | collective-permute-start | bytes 36872 | tf_op jit(solution)/shard_map/ppermute | solution.py:24
  175.0 13.1 %collective-permute-start.15 = (f32[3,2,1,512]{3,2,1,0:T(1,128)S(1)}, f32[3,2,1,512]{3,2,1,0:T(1,128)S(1)}, u32[]{:S(2)}, u32[]{:S(2)}) collective-permute-start(f32[3,2,1,512]{3,2,1,0:T(1,128)S(1)} %get-tuple-element.254), channel_id=1, source_target_pairs={{0,1},{1,2},{2,3},{3,4},{4,5},{5,6},{6,7},{8,9},{9,10},{10,11},{11... | collective-permute-start | bytes 36872 | tf_op jit(solution)/shard_map/ppermute | solution.py:21
  178.1 18.1 %copy-start.2 = (f32[3,2,16,512]{3,2,1,0:T(8,128)S(1)}, f32[3,2,16,512]{3,2,1,0:T(8,128)}, u32[]{:S(2)}) copy-start(f32[3,2,16,512]{3,2,1,0:T(8,128)} %param.19) | copy-start | bytes 589828
  178.1 18.1 %copy-start.6 = (f32[2,16,512]{2,1,0:T(8,128)S(1)}, f32[2,16,512]{2,1,0:T(8,128)}, u32[]{:S(2)}) copy-start(f32[2,16,512]{2,1,0:T(8,128)} %copy-done.5) | copy-start | bytes 196612
  178.1 18.1 %copy-start.8 = (f32[1,2,16,512]{3,2,1,0:T(8,128)S(1)}, f32[1,2,16,512]{3,2,1,0:T(8,128)}, u32[]{:S(2)}) copy-start(f32[1,2,16,512]{3,2,1,0:T(8,128)} %copy-done.7) | copy-start | bytes 196612
  178.1 18.0 %copy-start.17 = (f32[6,4,1,512]{3,2,1,0:T(1,128)S(1)}, f32[6,4,1,512]{3,2,1,0:T(1,128)}, u32[]{:S(2)}) copy-start(f32[6,4,1,512]{3,2,1,0:T(1,128)} %copy-done.16) | copy-start | bytes 147460
  178.1 18.0 %copy-start.19 = (f32[6,4,1,512]{3,2,1,0:T(1,128)S(1)}, f32[6,4,1,512]{3,2,1,0:T(1,128)}, u32[]{:S(2)}) copy-start(f32[6,4,1,512]{3,2,1,0:T(1,128)} %copy-done.18) | copy-start | bytes 147460
  178.1 11.3 %collective-permute-start.12 = (f32[3,1,16,512]{3,2,1,0:T(8,128)S(1)}, f32[3,1,16,512]{3,2,1,0:T(8,128)S(1)}, u32[]{:S(2)}, u32[]{:S(2)}) collective-permute-start(f32[3,1,16,512]{3,2,1,0:T(8,128)S(1)} %get-tuple-element.251), channel_id=1, source_target_pairs={{8,0},{16,8},{24,16},{9,1},{17,9},{25,17},{10,2},{18,10},{26,18},{... | collective-permute-start | bytes 294920 | tf_op jit(solution)/shard_map/ppermute | solution.py:24
  179.5 14.4 %collective-permute-start.13 = (f32[3,1,16,512]{3,2,1,0:T(8,128)S(1)}, f32[3,1,16,512]{3,2,1,0:T(8,128)S(1)}, u32[]{:S(2)}, u32[]{:S(2)}) collective-permute-start(f32[3,1,16,512]{3,2,1,0:T(8,128)S(1)} %get-tuple-element.252), channel_id=1, source_target_pairs={{0,8},{8,16},{16,24},{1,9},{9,17},{17,25},{2,10},{10,18},{18,26},{... | collective-permute-start | bytes 294920 | tf_op jit(solution)/shard_map/ppermute | solution.py:21
  186.7 8.1 %collective-permute-start.11 = (f32[3,2,1,512]{3,2,1,0:T(1,128)S(1)}, f32[3,2,1,512]{3,2,1,0:T(1,128)S(1)}, u32[]{:S(2)}, u32[]{:S(2)}) collective-permute-start(f32[3,2,1,512]{3,2,1,0:T(1,128)S(1)} %get-tuple-element.258), channel_id=1, source_target_pairs={{0,1},{1,2},{2,3},{3,4},{4,5},{5,6},{6,7},{8,9},{9,10},{10,11},{11... | collective-permute-start | bytes 36872 | tf_op jit(solution)/shard_map/ppermute | solution.py:21
  188.1 6.7 %collective-permute-start.8 = (f32[3,1,16,512]{3,2,1,0:T(8,128)S(1)}, f32[3,1,16,512]{3,2,1,0:T(8,128)S(1)}, u32[]{:S(2)}, u32[]{:S(2)}) collective-permute-start(f32[3,1,16,512]{3,2,1,0:T(8,128)S(1)} %get-tuple-element.255), channel_id=1, source_target_pairs={{8,0},{16,8},{24,16},{9,1},{17,9},{25,17},{10,2},{18,10},{26,18},{... | collective-permute-start | bytes 294920 | tf_op jit(solution)/shard_map/ppermute | solution.py:24
  189.4 6.8 %collective-permute-start.9 = (f32[3,1,16,512]{3,2,1,0:T(8,128)S(1)}, f32[3,1,16,512]{3,2,1,0:T(8,128)S(1)}, u32[]{:S(2)}, u32[]{:S(2)}) collective-permute-start(f32[3,1,16,512]{3,2,1,0:T(8,128)S(1)} %get-tuple-element.256), channel_id=1, source_target_pairs={{0,8},{8,16},{16,24},{1,9},{9,17},{17,25},{2,10},{10,18},{18,26},{... | collective-permute-start | bytes 294920 | tf_op jit(solution)/shard_map/ppermute | solution.py:21
  (45 other events, 31.9 us)
Sparse Core Ops, SparseCore 0:
  118.6 60.5 all-reduce.9
  184.3 44.6 all-reduce.11
